TPU v7x, 32 devices: a whole 2x2x4 slice. The times are simulated.
32 devices in a mesh: rows: 4 (over z), cent: 8 (over y, x, core).
Axes of the slice: x: 2, y: 2, z: 4, core: 2. Of those that a mesh axis runs over, the one named last changes fastest.
Arguments:
- train_rows: float32 [16384, 64], P('rows'), may hold values from -6 to 6
- centre_index: int32 [16384], P('cent'), may hold values from 0 to 16383
- precond: bfloat16 [16384, 16384], P('cent', 'rows'), as said below
- coefficients: float32 [16384, 128], P(('rows', 'cent')), may hold values from -6 to 6
- residual: float32 [16384, 128], P(('rows', 'cent')), may hold values from -6 to 6
- direction: float32 [16384, 128], P(('rows', 'cent')), may hold values from -6 to 6
Outputs:
- coef_next: float32 [16384, 128], P(('rows', 'cent'))
- residual_next: float32 [16384, 128], P(('rows', 'cent'))
- direction_next: float32 [16384, 128], P(('rows', 'cent'))
Inputs may be any that keep to these rules, and one draw needn't show every extreme that they name: precond is zero below its diagonal.
All inputs are finite; a program needn't handle non-finite values.
Results may differ from a plain program's by a relative error of at most 0.0047.
Values may be sent and summed in bfloat16 or wider, within the bound.
A program may use at most 128 MiB of HBM per device.

v0:
```python
import functools
import math

import jax
import jax.numpy as jnp
from jax import lax
from jax.experimental import pallas as pl
from jax.experimental.pallas import tpu as pltpu
from jax.sharding import PartitionSpec as P

FEAT = 64
OUTS = 128
CHUNK = 256
LAG = 3
F32 = jnp.float32
BF16 = jnp.bfloat16
MESH = pl.DeviceIdType.MESH
POINT_SCALE = math.sqrt(4.0 / FEAT)

ridge_weight = 0.1


def dot(a, b):
    return jnp.dot(a, b, preferred_element_type=F32)


def three(value):
    high = value.astype(BF16)
    rest = value - high.astype(F32)
    middle = rest.astype(BF16)
    low = (rest - middle.astype(F32)).astype(BF16)
    return high.astype(F32), middle.astype(F32), low.astype(F32)


def step_kernel(
    rows_n, cent_n,
    idx_ref, x_ref, p_hbm, res_ref, dir_ref,
    image_ref, sums_ref,
    p_buf, p_sem, k_buf, xaug, xhl_t, caug_t,
    pick, coef, grad, coef_low,
    dir_own, dir_all, fit_own, fit_all, gather_sems,
    fit_acc, fit_rs, img_acc, img_rs,
    sc_own, sc_cent, sc_mid, sc_rows, sc_sems,
):
    z = lax.axis_index("rows")
    me = lax.axis_index("cent")
    core = lax.rem(me, 2)
    chip = lax.div(me, 2)
    other = chip * 2 + (1 - core)
    chips = cent_n // 2
    chunks = p_buf.shape[0]
    rows_here = x_ref.shape[1]
    part = dir_own.shape[0]
    fit_part = fit_acc.shape[1]
    last = rows_n - 1

    def chip_at(distance):
        return lax.rem(chip + distance, chips)

    def p_copy(k):
        return pltpu.make_async_copy(
            p_hbm.at[pl.ds(pl.multiple_of(k * CHUNK, CHUNK), CHUNK)], p_buf.at[k], p_sem.at[k]
        )

    @pl.loop(0, chunks)
    def _(k):
        p_copy(k).start()

    barrier = pltpu.get_barrier_semaphore()
    for d in range(1, cent_n):
        pl.semaphore_signal(
            barrier, inc=1, device_id=(z, lax.rem(me + d, cent_n)), device_id_type=MESH
        )
    for d in range(1, rows_n):
        pl.semaphore_signal(
            barrier, inc=1, device_id=(lax.rem(z + d, rows_n), me), device_id_type=MESH
        )
    dir_own[...] = dir_ref[...].astype(BF16)
    pl.semaphore_wait(barrier, cent_n - 1 + rows_n - 1)

    def gather_copy(which, own, whole, d):
        target = other if d == 0 else chip_at(d) * 2 + core
        return pltpu.make_async_remote_copy(
            src_ref=own, dst_ref=whole.at[me],
            send_sem=gather_sems.at[which, 0, d], recv_sem=gather_sems.at[which, 1, d],
            device_id=(z, target), device_id_type=MESH,
        )

    def forward_copy(which, whole, d):
        source = chip_at(chips - d) * 2 + core
        return pltpu.make_async_remote_copy(
            src_ref=whole.at[source], dst_ref=whole.at[source],
            send_sem=gather_sems.at[which, 2, d], recv_sem=gather_sems.at[which, 3, d],
            device_id=(z, other), device_id_type=MESH,
        )

    def gather_start(which, own, whole):
        for d in list(range(1, chips)) + [0]:
            gather_copy(which, own, whole, d).start()
        whole[me] = own[...]

    def gather_forward(which, own, whole):
        for d in range(1, chips):
            gather_copy(which, own, whole, d).wait_recv()
            forward_copy(which, whole, d).start()

    def gather_end(which, own, whole):
        gather_copy(which, own, whole, 0).wait_recv()
        for d in range(1, chips):
            forward_copy(which, whole, d).wait_recv()
        for d in range(chips):
            gather_copy(which, own, whole, d).wait_send()
        for d in range(1, chips):
            forward_copy(which, whole, d).wait_send()

    def right_copy(scan, k):
        own, to_right, to_left, from_left, from_right, sems = scan
        return pltpu.make_async_remote_copy(
            src_ref=to_right.at[k], dst_ref=from_left.at[k],
            send_sem=sems.at[0, k], recv_sem=sems.at[1, k],
            device_id=(lax.rem(z + 1, rows_n), me), device_id_type=MESH,
        )

    def left_copy(scan, k):
        own, to_right, to_left, from_left, from_right, sems = scan
        return pltpu.make_async_remote_copy(
            src_ref=to_left.at[k], dst_ref=from_right.at[k],
            send_sem=sems.at[2, k], recv_sem=sems.at[3, k],
            device_id=(lax.rem(z + last, rows_n), me), device_id_type=MESH,
        )

    def scan_step(scan, it):
        own, to_right, to_left, from_left, from_right, sems = scan
        kr = it - LAG * z
        kl = it - LAG * (last - z)

        @pl.when((kr >= 0) & (kr < chunks) & (z < last))
        def _():
            @pl.when(z == 0)
            def _():
                to_right[kr] = own[kr].astype(BF16)

            @pl.when(z > 0)
            def _():
                right_copy(scan, kr).wait_recv()
                to_right[kr] = (own[kr].astype(F32) + from_left[kr].astype(F32)).astype(BF16)

            right_copy(scan, kr).start()

        @pl.when((kl >= 0) & (kl < chunks) & (z > 0))
        def _():
            @pl.when(z == last)
            def _():
                to_left[kl] = own[kl].astype(BF16)

            @pl.when(z < last)
            def _():
                left_copy(scan, kl).wait_recv()
                to_left[kl] = (own[kl].astype(F32) + from_right[kl].astype(F32)).astype(BF16)

            left_copy(scan, kl).start()

    def scan_total(scan, k):
        own, to_right, to_left, from_left, from_right, sems = scan

        @pl.when(z == last)
        def _():
            right_copy(scan, k).wait_recv()

        @pl.when(z == 0)
        def _():
            left_copy(scan, k).wait_recv()

        @pl.when(z > 0)
        def _():
            own[k] = (own[k].astype(F32) + from_left[k].astype(F32)).astype(own.dtype)

        @pl.when(z < last)
        def _():
            own[k] = (own[k].astype(F32) + from_right[k].astype(F32)).astype(own.dtype)

    def scan_sent(scan):
        @pl.loop(0, chunks)
        def _(k):
            @pl.when(z < last)
            def _():
                right_copy(scan, k).wait_send()

            @pl.when(z > 0)
            def _():
                left_copy(scan, k).wait_send()

    def across_copy(buffers, h, q):
        send_a, recv_a, send_b, recv_b, sems = buffers
        return pltpu.make_async_remote_copy(
            src_ref=send_a.at[h, q], dst_ref=recv_a.at[h, q],
            send_sem=sems.at[h, 0, q], recv_sem=sems.at[h, 1, q],
            device_id=(z, other), device_id_type=MESH,
        )

    def between_copy(buffers, h, d):
        send_a, recv_a, send_b, recv_b, sems = buffers
        return pltpu.make_async_remote_copy(
            src_ref=send_b.at[h, d], dst_ref=recv_b.at[h, d],
            send_sem=sems.at[h, 2, d], recv_sem=sems.at[h, 3, d],
            device_id=(z, chip_at(d) * 2 + core), device_id_type=MESH,
        )

    def scatter_start(mine, buffers):
        send_a, recv_a, send_b, recv_b, sems = buffers
        for h in range(send_a.shape[0]):
            for d in list(range(1, chips)) + [0]:
                q = chip_at(d)
                send_a[h, q] = mine(h, q * 2 + (1 - core)).astype(BF16)
                across_copy(buffers, h, q).start()
        for h in range(send_a.shape[0]):
            for d in range(1, chips):
                q = chip_at(d)
                across_copy(buffers, h, q).wait_recv()
                send_b[h, d] = (mine(h, q * 2 + core) + recv_a[h, q].astype(F32)).astype(BF16)
                between_copy(buffers, h, d).start()

    def scatter_end(mine, buffers, h):
        send_a, recv_a, send_b, recv_b, sems = buffers
        across_copy(buffers, h, chip).wait_recv()
        total = mine(h, me) + recv_a[h, chip].astype(F32)
        for d in range(1, chips):
            between_copy(buffers, h, d).wait_recv()
            total = total + recv_b[h, d].astype(F32)
        return total

    def scatter_sent(buffers):
        for h in range(buffers[0].shape[0]):
            for d in range(chips):
                across_copy(buffers, h, chip_at(d)).wait_send()
            for d in range(1, chips):
                between_copy(buffers, h, d).wait_send()

    gather_start(0, dir_own, dir_all)

    point_block = rows_here // chunks

    for b in range(chunks):
        here = slice(b * point_block, (b + 1) * point_block)
        points = x_ref[:, here] * POINT_SCALE
        high = points.astype(BF16)
        xhl_t[:FEAT, here] = high
        xhl_t[FEAT:, here] = (points - high.astype(F32)).astype(BF16)

    def augmented(pair, norm_at, one_at):
        high = pair[:FEAT]
        low = pair[FEAT:]
        exact = high + low
        half = -0.5 * jnp.sum(exact * exact, axis=0, keepdims=True)
        sub = lax.broadcasted_iota(jnp.int32, high.shape, 0)
        extra = jnp.where((sub >= one_at) & (sub < one_at + 3), 1.0, 0.0)
        for at, term in enumerate(three(half)):
            extra = jnp.where(sub == norm_at + at, term, extra)
        return high, low, extra

    def augment(b):
        here = pl.ds(pl.multiple_of(b * point_block, point_block), point_block)
        high, low, extra = augmented(xhl_t[:, here].astype(F32), 0, 3)
        xaug[here, :] = jnp.concatenate([high, low, high, extra], axis=0).T.astype(BF16)

    pick_block = math.gcd(rows_here, 1024)

    @pl.loop(0, chunks)
    def _(it):
        wanted = idx_ref[it] - z * rows_here
        total = jnp.zeros((2 * FEAT, CHUNK), F32)
        for b in range(rows_here // pick_block):
            ids = lax.broadcasted_iota(jnp.int32, (pick_block, CHUNK), 0) + b * pick_block
            hot = jnp.where(ids == wanted, 1.0, 0.0).astype(BF16)
            total = total + dot(xhl_t[:, b * pick_block : (b + 1) * pick_block], hot)
        pick[0][it] = total.astype(BF16)
        scan_step(pick, it)
        augment(it)

    gather_forward(0, dir_own, dir_all)
    gather_end(0, dir_own, dir_all)

    fit_acc[...] = jnp.zeros_like(fit_acc)
    k_block = math.gcd(rows_here, 512)

    @pl.loop(0, chunks + LAG * last)
    def _(it):
        scan_step(pick, it + chunks)

        @pl.when(it < chunks)
        def _():
            p_copy(it).wait()
            directions = dir_all[...].reshape(cent_n * part, OUTS)
            coef[0][it] = dot(p_buf[it], directions)

        scan_step(coef, it)

        @pl.when(it < chunks)
        def _():
            scan_total(pick, it)
            high, low, extra = augmented(pick[0][it].astype(F32), 3, 0)
            caug_t[...] = jnp.concatenate([high, high, low, extra], axis=0).astype(BF16)

            for b in range(rows_here // k_block):
                here = slice(b * k_block, (b + 1) * k_block)
                k_buf[it, here, :] = jnp.exp(dot(xaug[here, :], caug_t[...])).astype(BF16)

        @pl.when(it >= LAG * last)
        def _():
            k = it - LAG * last
            scan_total(coef, k)
            coef_low[...] = coef[0][k].astype(BF16)

            for b in range(cent_n):
                here = slice(b * fit_part, (b + 1) * fit_part)
                fit_acc[b] += dot(k_buf[k, here, :], coef_low[...])

    fit_pieces = fit_own.shape[0]
    fit_piece = fit_part // fit_pieces

    def fit_mine(h, block):
        return fit_acc[block, h * fit_piece : (h + 1) * fit_piece, :]

    scatter_start(fit_mine, fit_rs)
    for h in range(fit_pieces):
        fit_own[h] = scatter_end(fit_mine, fit_rs, h).T.astype(BF16)
        gather_start(1 + h, fit_own.at[h], fit_all.at[h])
    img_acc[...] = jnp.zeros_like(img_acc)
    for h in range(fit_pieces):
        gather_forward(1 + h, fit_own.at[h], fit_all.at[h])
    for h in range(fit_pieces):
        gather_end(1 + h, fit_own.at[h], fit_all.at[h])
    scatter_sent(fit_rs)

    scale = float(rows_here * rows_n) ** -0.5

    @pl.loop(0, chunks + LAG * last)
    def _(it):
        @pl.when(it < chunks)
        def _():
            total = jnp.zeros((OUTS, CHUNK), F32)
            for b in range(cent_n):
                for h in range(fit_pieces):
                    start = b * fit_part + h * fit_piece
                    total = total + dot(fit_all[h, b], k_buf[it, start : start + fit_piece, :])
            grad[0][it] = total

        scan_step(grad, it)

        @pl.when(it >= LAG * last)
        def _():
            k = it - LAG * last
            scan_total(grad, k)
            low = (grad[0][k] * scale).astype(BF16)
            for b in range(cent_n):
                img_acc[b] += dot(low, p_buf[k, :, b * part : (b + 1) * part])

    img_pieces = img_rs[0].shape[0]
    img_piece = part // img_pieces

    def img_mine(h, block):
        return img_acc[block, :, h * img_piece : (h + 1) * img_piece]

    scatter_start(img_mine, img_rs)
    image = jnp.concatenate(
        [scatter_end(img_mine, img_rs, h).T for h in range(img_pieces)], axis=0
    )
    image = image + ridge_weight * dir_ref[...]
    image_ref[...] = image

    def rows_sum(value):
        return jnp.sum(value, axis=0, keepdims=True)

    residual = res_ref[...]
    sc_own[...] = jnp.concatenate(
        [
            rows_sum(residual * residual),
            rows_sum(dir_ref[...] * image),
            rows_sum(residual * image),
            rows_sum(image * image),
            jnp.zeros((4, OUTS), F32),
        ],
        axis=0,
    )

    def cent_copy(d):
        return pltpu.make_async_remote_copy(
            src_ref=sc_own, dst_ref=sc_cent.at[d],
            send_sem=sc_sems.at[0, d], recv_sem=sc_sems.at[1, d],
            device_id=(z, lax.rem(me + d, cent_n)), device_id_type=MESH,
        )

    def rows_copy(d):
        return pltpu.make_async_remote_copy(
            src_ref=sc_mid, dst_ref=sc_rows.at[d],
            send_sem=sc_sems.at[2, d], recv_sem=sc_sems.at[3, d],
            device_id=(lax.rem(z + d, rows_n), me), device_id_type=MESH,
        )

    for d in range(1, cent_n):
        cent_copy(d).start()
    total = sc_own[...]
    for d in range(1, cent_n):
        cent_copy(d).wait_recv()
        total = total + sc_cent[d]
    sc_mid[...] = total
    for d in range(1, rows_n):
        rows_copy(d).start()
    for d in range(1, rows_n):
        rows_copy(d).wait_recv()
        total = total + sc_rows[d]
    sums_ref[...] = total

    for d in range(1, cent_n):
        cent_copy(d).wait_send()
    for d in range(1, rows_n):
        rows_copy(d).wait_send()
    scan_sent(pick)
    scan_sent(coef)
    scan_sent(grad)
    scatter_sent(img_rs)


def update_kernel(sums_ref, image_ref, coef_ref, res_ref, dir_ref, coef_out, res_out, dir_out):
    totals = jnp.sum(sums_ref[...], axis=1, keepdims=True)
    norm_old, curvature, cross, square = (totals[at : at + 1] for at in range(4))
    step_size = norm_old / curvature
    norm_new = norm_old - 2.0 * step_size * cross + step_size * step_size * square
    ratio = norm_new / norm_old
    direction = dir_ref[...]
    coef_out[...] = coef_ref[...] + step_size * direction
    residual_next = res_ref[...] - step_size * image_ref[...]
    res_out[...] = residual_next
    dir_out[...] = residual_next + ratio * direction


def on_device(rows_n, cent_n, train_rows, centre_index, precond, coefficients, residual, direction):
    rows_here = train_rows.shape[0]
    centres_here = centre_index.shape[0]
    part = direction.shape[0]
    chunks = centres_here // CHUNK
    chips = cent_n // 2
    fit_part = rows_here // cent_n
    fit_pieces = 2 if fit_part % 256 == 0 else 1
    img_pieces = 2 if part % 256 == 0 else 1
    vmem = pl.BlockSpec(memory_space=pltpu.VMEM)

    def scan(shape, own_dtype):
        piece = (chunks,) + shape
        return (
            pltpu.VMEM(piece, own_dtype),
            pltpu.VMEM(piece, BF16), pltpu.VMEM(piece, BF16),
            pltpu.VMEM(piece, BF16), pltpu.VMEM(piece, BF16),
            pltpu.SemaphoreType.DMA((4, chunks)),
        )

    def scatter(pieces, shape):
        piece = (pieces, chips) + shape
        return (
            pltpu.VMEM(piece, BF16), pltpu.VMEM(piece, BF16),
            pltpu.VMEM(piece, BF16), pltpu.VMEM(piece, BF16),
            pltpu.SemaphoreType.DMA((pieces, 4, chips)),
        )

    image, sums = pl.pallas_call(
        functools.partial(step_kernel, rows_n, cent_n),
        out_shape=(
            jax.ShapeDtypeStruct((part, OUTS), F32),
            jax.ShapeDtypeStruct((8, OUTS), F32),
        ),
        in_specs=[vmem, vmem, pl.BlockSpec(memory_space=pl.ANY), vmem, vmem],
        out_specs=(vmem, vmem),
        scratch_shapes=[
            pltpu.VMEM((chunks, CHUNK, precond.shape[1]), BF16),
            pltpu.SemaphoreType.DMA((chunks,)),
            pltpu.VMEM((chunks, rows_here, CHUNK), BF16),
            pltpu.VMEM((rows_here, 4 * FEAT), BF16),
            pltpu.VMEM((2 * FEAT, rows_here), BF16),
            pltpu.VMEM((4 * FEAT, CHUNK), BF16),
            scan((2 * FEAT, CHUNK), BF16),
            scan((CHUNK, OUTS), F32),
            scan((OUTS, CHUNK), F32),
            pltpu.VMEM((CHUNK, OUTS), BF16),
            pltpu.VMEM((part, OUTS), BF16),
            pltpu.VMEM((cent_n, part, OUTS), BF16),
            pltpu.VMEM((fit_pieces, OUTS, fit_part // fit_pieces), BF16),
            pltpu.VMEM((fit_pieces, cent_n, OUTS, fit_part // fit_pieces), BF16),
            pltpu.SemaphoreType.DMA((1 + fit_pieces, 4, chips)),
            pltpu.VMEM((cent_n, fit_part, OUTS), F32),
            scatter(fit_pieces, (fit_part // fit_pieces, OUTS)),
            pltpu.VMEM((cent_n, OUTS, part), F32),
            scatter(img_pieces, (OUTS, part // img_pieces)),
            pltpu.VMEM((8, OUTS), F32),
            pltpu.VMEM((cent_n, 8, OUTS), F32),
            pltpu.VMEM((8, OUTS), F32),
            pltpu.VMEM((rows_n, 8, OUTS), F32),
            pltpu.SemaphoreType.DMA((4, max(cent_n, rows_n))),
        ],
        compiler_params=pltpu.CompilerParams(
            collective_id=0, has_side_effects=True, vmem_limit_bytes=67000000
        ),
        name="falkon_step",
    )(centre_index.reshape(chunks, 1, CHUNK), train_rows.T, precond, residual, direction)

    piece = jax.ShapeDtypeStruct((part, OUTS), F32)
    return pl.pallas_call(
        update_kernel,
        out_shape=(piece, piece, piece),
        in_specs=[vmem] * 5,
        out_specs=(vmem, vmem, vmem),
        name="falkon_update",
    )(sums, image, coefficients, residual, direction)


def solution(mesh):
    both = P(("rows", "cent"), None)
    return jax.shard_map(
        functools.partial(on_device, mesh.shape["rows"], mesh.shape["cent"]),
        mesh=mesh,
        in_specs=(P("rows", None), P("cent"), P("cent", "rows"), both, both, both),
        out_specs=(both, both, both),
        check_vma=False,
    )
```

profile of v0, /device:TPU:0, one launch (start us, length us, event | category | flops | bytes accessed | tf_op | source)
XLA Modules:
  0.0 101.2 jit_solution(13078048184235383308)
XLA Ops:
  0.6 98.3 %falkon_step.1 = (f32[512,128]{1,0:T(8,128)}, f32[8,128]{1,0:T(8,128)}) custom-call(s32[8,1,256]{2,1,0:T(1,128)} %bitcast.3, f32[64,4096]{1,0:T(8,128)} %bitcast.2, bf16[2048,4096]{1,0:T(8,128)(2,1)} %p_hbm.1, f32[512,128]{1,0:T(8,128)} %res_ref.3, f32[512,128]{1,0:T(8,128)} %dir_ref.3), custom_call_target="tpu_custom_call" | custom-call | tf_op jit(solution)/shard_map/falkon_step/pallas_call | solution.py:465
  99.0 2.2 %falkon_update.1 = (f32[512,128]{1,0:T(8,128)}, f32[512,128]{1,0:T(8,128)}, f32[512,128]{1,0:T(8,128)}) custom-call(f32[8,128]{1,0:T(8,128)} %get-tuple-element.5.sums_ref, f32[512,128]{1,0:T(8,128)} %get-tuple-element.6.image_ref, f32[512,128]{1,0:T(8,128)} %coef_ref.1, f32[512,128]{1,0:T(8,128)} %res_ref.3, f32[512,128]{1,0:T(8,128)} %dir_ref.3), custom_call_target="tpu_custom_call" | custom-call | tf_op jit(solution)/shard_map/falkon_update/pallas_call | solution.py:506
where the time goes:
time: 101 us
  Pallas kernels  101 us (100%)
    pallas_call x1, Pallas kernels, on_device(): pl.pallas_call(functools.partial(step_kernel, rows_n, cent_n), out_shape=...  98.3 us
    pallas_call x1, Pallas kernels, on_device(): pl.pallas_call(update_kernel, out_shape=(piece, piece, piece), in_specs=[...  2.22 us

commit v1 on v0

v1 whole, which is shorter than its diff:
```python
import functools
import math

import jax
import jax.numpy as jnp
from jax import lax
from jax.experimental import pallas as pl
from jax.experimental.pallas import tpu as pltpu
from jax.sharding import PartitionSpec as P

FEAT = 64
OUTS = 128
CHUNK = 256
GROUPS = 2
LAG = 4
COEF_AT = 10
BUILD_AFTER = 8
WIDEST = 6.0
F32 = jnp.float32
BF16 = jnp.bfloat16
I16 = jnp.int16
I32 = jnp.int32
MESH = pl.DeviceIdType.MESH
STEPS = 5461.0
LOG2E = math.log2(math.e)
CROSS = LOG2E * 4.0 / FEAT / STEPS
POINT_NORM = -STEPS * STEPS * FEAT / (8.0 * LOG2E)
CENTRE_NORM = -LOG2E * 2.0 / FEAT / (STEPS * STEPS)

ridge_weight = 0.1


def dot(a, b):
    return jnp.dot(a, b, preferred_element_type=F32)


def dot_t(a, b):
    return lax.dot_general(a, b, (((1,), (1,)), ((), ())), preferred_element_type=F32)


def three(value):
    high = value.astype(BF16)
    rest = value - high.astype(F32)
    middle = rest.astype(BF16)
    low = (rest - middle.astype(F32)).astype(BF16)
    return high.astype(F32), middle.astype(F32), low.astype(F32)


def augmented(high, low, norm_scale, norm_at, one_at):
    exact = high + low
    norm = norm_scale * jnp.sum(exact * exact, axis=0, keepdims=True)
    sub = lax.broadcasted_iota(I32, high.shape, 0)
    extra = jnp.where((sub >= one_at) & (sub < one_at + 3), 1.0, 0.0)
    for at, term in enumerate(three(norm)):
        extra = jnp.where(sub == norm_at + at, term, extra)
    return extra


def step_kernel(
    rows_n, cent_n,
    idx_ref, x_ref, p_hbm, res_ref, dir_ref,
    image_ref, sums_ref,
    p_buf, p_sem, kt_buf, xaug_t, nhl_t,
    pick, coef, grad,
    dir_own, dir_all, fit_own, fit_all, gather_sems,
    fit_acc, fit_rs, img_acc, img_rs,
    sc_own, sc_cent, sc_mid, sc_rows, sc_sems,
):
    z = lax.axis_index("rows")
    me = lax.axis_index("cent")
    core = lax.rem(me, 2)
    chip = lax.div(me, 2)
    other = chip * 2 + (1 - core)
    chips = cent_n // 2
    chunks = p_buf.shape[0]
    rows_here = x_ref.shape[1]
    part = dir_own.shape[1]
    fit_part = fit_acc.shape[3]
    group = OUTS // GROUPS
    items = GROUPS * chunks
    last = rows_n - 1
    reach = LAG * last

    def chip_at(distance):
        return lax.rem(chip + distance, chips)

    def p_copy(k):
        return pltpu.make_async_copy(
            p_hbm.at[pl.ds(pl.multiple_of(k * CHUNK, CHUNK), CHUNK)], p_buf.at[k], p_sem.at[k]
        )

    barrier = pltpu.get_barrier_semaphore()
    for d in range(1, cent_n):
        pl.semaphore_signal(
            barrier, inc=1, device_id=(z, lax.rem(me + d, cent_n)), device_id_type=MESH
        )
    for d in range(1, rows_n):
        pl.semaphore_signal(
            barrier, inc=1, device_id=(lax.rem(z + d, rows_n), me), device_id_type=MESH
        )

    @pl.loop(0, chunks)
    def _(k):
        p_copy(k).start()

    dir_own[...] = dir_ref[...].T.astype(BF16)
    for scan in (pick, coef, grad):
        @pl.when(z == 0)
        def _():
            scan[3][...] = jnp.zeros_like(scan[3])

        @pl.when(z == last)
        def _():
            scan[4][...] = jnp.zeros_like(scan[4])

    pl.semaphore_wait(barrier, cent_n - 1 + rows_n - 1)

    def gather_copy(which, own, whole, d):
        target = other if d == 0 else chip_at(d) * 2 + core
        return pltpu.make_async_remote_copy(
            src_ref=own, dst_ref=whole.at[me],
            send_sem=gather_sems.at[which, 0, d], recv_sem=gather_sems.at[which, 1, d],
            device_id=(z, target), device_id_type=MESH,
        )

    def forward_copy(which, whole, d):
        source = chip_at(chips - d) * 2 + core
        return pltpu.make_async_remote_copy(
            src_ref=whole.at[source], dst_ref=whole.at[source],
            send_sem=gather_sems.at[which, 2, d], recv_sem=gather_sems.at[which, 3, d],
            device_id=(z, other), device_id_type=MESH,
        )

    def gather_start(which, own, whole):
        for d in list(range(1, chips)) + [0]:
            gather_copy(which, own, whole, d).start()
        whole[me] = own[...]

    def gather_forward(which, own, whole):
        for d in range(1, chips):
            gather_copy(which, own, whole, d).wait_recv()
            forward_copy(which, whole, d).start()

    def gather_end(which, own, whole):
        gather_copy(which, own, whole, 0).wait_recv()
        for d in range(1, chips):
            forward_copy(which, whole, d).wait_recv()

    def gather_sent(which, own, whole):
        for d in range(chips):
            gather_copy(which, own, whole, d).wait_send()
        for d in range(1, chips):
            forward_copy(which, whole, d).wait_send()

    def right_copy(scan, k):
        own, to_right, to_left, from_left, from_right, sems = scan
        return pltpu.make_async_remote_copy(
            src_ref=to_right.at[k], dst_ref=from_left.at[k],
            send_sem=sems.at[0, k], recv_sem=sems.at[1, k],
            device_id=(lax.rem(z + 1, rows_n), me), device_id_type=MESH,
        )

    def left_copy(scan, k):
        own, to_right, to_left, from_left, from_right, sems = scan
        return pltpu.make_async_remote_copy(
            src_ref=to_left.at[k], dst_ref=from_right.at[k],
            send_sem=sems.at[2, k], recv_sem=sems.at[3, k],
            device_id=(lax.rem(z + last, rows_n), me), device_id_type=MESH,
        )

    def wide(scan):
        return I32 if scan[0].dtype == I16 else F32

    def scan_step(scan, it):
        own, to_right, to_left, from_left, from_right, sems = scan
        kr = it - LAG * z
        kl = it - LAG * (last - z)
        kind = wide(scan)

        @pl.when((kr >= 0) & (kr < own.shape[0]) & (z < last))
        def _():
            @pl.when(z > 0)
            def _():
                right_copy(scan, kr).wait_recv()

            to_right[kr] = (own[kr].astype(kind) + from_left[kr].astype(kind)).astype(to_right.dtype)
            right_copy(scan, kr).start()

        @pl.when((kl >= 0) & (kl < own.shape[0]) & (z > 0))
        def _():
            @pl.when(z < last)
            def _():
                left_copy(scan, kl).wait_recv()

            to_left[kl] = (own[kl].astype(kind) + from_right[kl].astype(kind)).astype(to_left.dtype)
            left_copy(scan, kl).start()

    def scan_total(scan, k):
        own, to_right, to_left, from_left, from_right, sems = scan
        kind = wide(scan)

        @pl.when(z == last)
        def _():
            right_copy(scan, k).wait_recv()

        @pl.when(z == 0)
        def _():
            left_copy(scan, k).wait_recv()

        return own[k].astype(kind) + from_left[k].astype(kind) + from_right[k].astype(kind)

    def scan_sent(scan):
        @pl.loop(0, scan[0].shape[0])
        def _(k):
            @pl.when(z < last)
            def _():
                right_copy(scan, k).wait_send()

            @pl.when(z > 0)
            def _():
                left_copy(scan, k).wait_send()

    def across_copy(buffers, g, q):
        send_a, recv_a, send_b, recv_b, sems = buffers
        return pltpu.make_async_remote_copy(
            src_ref=send_a.at[g, q], dst_ref=recv_a.at[g, q],
            send_sem=sems.at[g, 0, q], recv_sem=sems.at[g, 1, q],
            device_id=(z, other), device_id_type=MESH,
        )

    def between_copy(buffers, g, d):
        send_a, recv_a, send_b, recv_b, sems = buffers
        return pltpu.make_async_remote_copy(
            src_ref=send_b.at[g, d], dst_ref=recv_b.at[g, d],
            send_sem=sems.at[g, 2, d], recv_sem=sems.at[g, 3, d],
            device_id=(z, chip_at(d) * 2 + core), device_id_type=MESH,
        )

    def scatter_across(acc, buffers, g):
        for d in list(range(1, chips)) + [0]:
            q = chip_at(d)
            buffers[0][g, q] = acc[g, q * 2 + (1 - core)].astype(BF16)
            across_copy(buffers, g, q).start()

    def scatter_between(acc, buffers, g):
        send_a, recv_a, send_b, recv_b, sems = buffers
        for d in range(1, chips):
            q = chip_at(d)
            across_copy(buffers, g, q).wait_recv()
            send_b[g, d] = (acc[g, q * 2 + core] + recv_a[g, q].astype(F32)).astype(BF16)
            between_copy(buffers, g, d).start()

    def scatter_end(acc, buffers, g):
        send_a, recv_a, send_b, recv_b, sems = buffers
        across_copy(buffers, g, chip).wait_recv()
        total = acc[g, me] + recv_a[g, chip].astype(F32)
        for d in range(1, chips):
            between_copy(buffers, g, d).wait_recv()
            total = total + recv_b[g, d].astype(F32)
        return total

    def scatter_sent(buffers):
        for g in range(GROUPS):
            for d in range(chips):
                across_copy(buffers, g, chip_at(d)).wait_send()
            for d in range(1, chips):
                between_copy(buffers, g, d).wait_send()

    gather_start(0, dir_own, dir_all)

    x_block = rows_here // chunks
    for b in range(chunks):
        here = slice(b * x_block, (b + 1) * x_block)
        number = jnp.round(x_ref[:, here] * STEPS)
        high = number.astype(BF16)
        nhl_t[:FEAT, here] = high
        nhl_t[FEAT:, here] = (number - high.astype(F32)).astype(BF16)

    def augment_points(b):
        here = pl.ds(pl.multiple_of(b * x_block, x_block), x_block)
        points = x_ref[:, here] * CROSS
        high = points.astype(BF16).astype(F32)
        low = (points - high).astype(BF16).astype(F32)
        extra = augmented(high, low, POINT_NORM, 0, 3)
        for at, term in enumerate((high, low, high, extra)):
            xaug_t[at * FEAT : (at + 1) * FEAT, here] = term.astype(BF16)

    pick_block = math.gcd(rows_here, 1024)

    def pick_own(k):
        wanted = idx_ref[k] - z * rows_here
        total = jnp.zeros((2 * FEAT, CHUNK), F32)
        for b in range(rows_here // pick_block):
            ids = lax.broadcasted_iota(I32, (pick_block, CHUNK), 0) + b * pick_block
            hot = jnp.where(ids == wanted, 1.0, 0.0).astype(BF16)
            total = total + dot(nhl_t[:, b * pick_block : (b + 1) * pick_block], hot)
        pick[0][k] = (total[:FEAT] + total[FEAT:]).astype(I32).astype(I16)

    def coef_own(k):
        p_copy(k).wait()
        total = jnp.zeros((OUTS, CHUNK), F32)
        for b in range(cent_n):
            total = total + dot_t(dir_all[b], p_buf[k, :, b * part : (b + 1) * part])
        for g in range(GROUPS):
            coef[0][g * chunks + k] = total[g * group : (g + 1) * group]

    k_block = math.gcd(rows_here, 512)

    def build(k):
        number = scan_total(pick, k).astype(F32)
        high = number.astype(BF16).astype(F32)
        low = number - high
        extra = augmented(high, low, CENTRE_NORM, 3, 0)
        caug = jnp.concatenate([high, high, low, extra], axis=0).T.astype(BF16)
        for b in range(rows_here // k_block):
            here = slice(b * k_block, (b + 1) * k_block)
            kt_buf[k, :, here] = jnp.exp2(dot(caug, xaug_t[:, here])).astype(BF16)

    def fit_add(i):
        g = lax.div(i, chunks)
        k = lax.rem(i, chunks)
        low = scan_total(coef, i).astype(BF16)
        for b in range(cent_n):
            fit_acc[g, b] += dot(low, kt_buf[k, :, b * fit_part : (b + 1) * fit_part])

    fit_acc[...] = jnp.zeros_like(fit_acc)
    img_acc[...] = jnp.zeros_like(img_acc)
    build_at = COEF_AT + BUILD_AFTER
    fit_at = COEF_AT + reach

    @pl.loop(0, fit_at + items)
    def _(it):
        @pl.when(it < chunks)
        def _():
            pick_own(it)

        scan_step(pick, it)

        @pl.when(it < chunks)
        def _():
            augment_points(it)

        @pl.when(it == COEF_AT)
        def _():
            gather_forward(0, dir_own, dir_all)
            gather_end(0, dir_own, dir_all)

        @pl.when((it >= COEF_AT) & (it < COEF_AT + chunks))
        def _():
            coef_own(it - COEF_AT)

        scan_step(coef, it - COEF_AT)

        @pl.when((it >= build_at) & (it < build_at + chunks))
        def _():
            build(it - build_at)

        @pl.when(it >= fit_at)
        def _():
            fit_add(it - fit_at)

        for g in range(GROUPS):
            done = fit_at + (g + 1) * chunks - 1

            @pl.when(it == done)
            def _():
                scatter_across(fit_acc, fit_rs, g)

            if g < GROUPS - 1:
                @pl.when(it == done + 2)
                def _():
                    scatter_between(fit_acc, fit_rs, g)

    def fit_shared(g):
        fit_own[g] = scatter_end(fit_acc, fit_rs, g).astype(BF16)
        gather_start(1 + g, fit_own.at[g], fit_all.at[g])

    for g in range(GROUPS - 1):
        fit_shared(g)
    scatter_between(fit_acc, fit_rs, GROUPS - 1)
    for g in range(GROUPS - 1):
        gather_forward(1 + g, fit_own.at[g], fit_all.at[g])
    fit_shared(GROUPS - 1)
    gather_end(1, fit_own.at[0], fit_all.at[0])

    scale = float(rows_here * rows_n) ** -0.5

    def grad_own(i):
        g = lax.div(i, chunks)
        k = lax.rem(i, chunks)
        total = jnp.zeros((group, CHUNK), F32)
        for b in range(cent_n):
            total = total + dot_t(fit_all[g, b], kt_buf[k, :, b * fit_part : (b + 1) * fit_part])
        grad[0][i] = total

    def img_add(i):
        g = lax.div(i, chunks)
        k = lax.rem(i, chunks)
        low = (scan_total(grad, i) * scale).astype(BF16)
        for b in range(cent_n):
            img_acc[g, b] += dot(low, p_buf[k, :, b * part : (b + 1) * part])

    @pl.loop(0, items + reach)
    def _(it):
        for g in range(1, GROUPS):
            @pl.when(it == g * chunks)
            def _():
                if g == GROUPS - 1:
                    gather_forward(1 + g, fit_own.at[g], fit_all.at[g])
                gather_end(1 + g, fit_own.at[g], fit_all.at[g])

        @pl.when(it < items)
        def _():
            grad_own(it)

        scan_step(grad, it)

        @pl.when(it >= reach)
        def _():
            img_add(it - reach)

        for g in range(GROUPS):
            done = reach + (g + 1) * chunks - 1

            @pl.when(it == done)
            def _():
                scatter_across(img_acc, img_rs, g)

            if g < GROUPS - 1:
                @pl.when(it == done + 2)
                def _():
                    scatter_between(img_acc, img_rs, g)

    images = [scatter_end(img_acc, img_rs, g) for g in range(GROUPS - 1)]
    scatter_between(img_acc, img_rs, GROUPS - 1)
    images.append(scatter_end(img_acc, img_rs, GROUPS - 1))
    image = jnp.concatenate(images, axis=0).T
    image = image + ridge_weight * dir_ref[...]
    image_ref[...] = image

    def rows_sum(value):
        return jnp.sum(value, axis=0, keepdims=True)

    residual = res_ref[...]
    sc_own[...] = jnp.concatenate(
        [
            rows_sum(residual * residual),
            rows_sum(dir_ref[...] * image),
            rows_sum(residual * image),
            rows_sum(image * image),
            jnp.zeros((4, OUTS), F32),
        ],
        axis=0,
    )

    def cent_copy(d):
        return pltpu.make_async_remote_copy(
            src_ref=sc_own, dst_ref=sc_cent.at[d],
            send_sem=sc_sems.at[0, d], recv_sem=sc_sems.at[1, d],
            device_id=(z, lax.rem(me + d, cent_n)), device_id_type=MESH,
        )

    def rows_copy(d):
        return pltpu.make_async_remote_copy(
            src_ref=sc_mid, dst_ref=sc_rows.at[d],
            send_sem=sc_sems.at[2, d], recv_sem=sc_sems.at[3, d],
            device_id=(lax.rem(z + d, rows_n), me), device_id_type=MESH,
        )

    for d in range(1, cent_n):
        cent_copy(d).start()
    total = sc_own[...]
    for d in range(1, cent_n):
        cent_copy(d).wait_recv()
        total = total + sc_cent[d]
    sc_mid[...] = total
    for d in range(1, rows_n):
        rows_copy(d).start()
    gather_sent(0, dir_own, dir_all)
    for g in range(GROUPS):
        gather_sent(1 + g, fit_own.at[g], fit_all.at[g])
    scatter_sent(fit_rs)
    scatter_sent(img_rs)
    scan_sent(pick)
    scan_sent(coef)
    scan_sent(grad)
    for d in range(1, cent_n):
        cent_copy(d).wait_send()
    for d in range(1, rows_n):
        rows_copy(d).wait_recv()
        total = total + sc_rows[d]
    sums_ref[...] = total
    for d in range(1, rows_n):
        rows_copy(d).wait_send()


def update_kernel(sums_ref, image_ref, coef_ref, res_ref, dir_ref, coef_out, res_out, dir_out):
    totals = jnp.sum(sums_ref[...], axis=1, keepdims=True)
    norm_old, curvature, cross, square = (totals[at : at + 1] for at in range(4))
    step_size = norm_old / curvature
    norm_new = norm_old - 2.0 * step_size * cross + step_size * step_size * square
    ratio = norm_new / norm_old
    direction = dir_ref[...]
    coef_out[...] = coef_ref[...] + step_size * direction
    residual_next = res_ref[...] - step_size * image_ref[...]
    res_out[...] = residual_next
    dir_out[...] = residual_next + ratio * direction


def on_device(rows_n, cent_n, train_rows, centre_index, precond, coefficients, residual, direction):
    rows_here = train_rows.shape[0]
    centres_here = centre_index.shape[0]
    part = direction.shape[0]
    chunks = centres_here // CHUNK
    chips = cent_n // 2
    fit_part = rows_here // cent_n
    group = OUTS // GROUPS
    vmem = pl.BlockSpec(memory_space=pltpu.VMEM)

    def scan(count, shape, own_dtype, link_dtype):
        piece = (count,) + shape
        return (
            pltpu.VMEM(piece, own_dtype),
            pltpu.VMEM(piece, link_dtype), pltpu.VMEM(piece, link_dtype),
            pltpu.VMEM(piece, link_dtype), pltpu.VMEM(piece, link_dtype),
            pltpu.SemaphoreType.DMA((4, count)),
        )

    def scatter(shape):
        piece = (GROUPS, chips) + shape
        return (
            pltpu.VMEM(piece, BF16), pltpu.VMEM(piece, BF16),
            pltpu.VMEM(piece, BF16), pltpu.VMEM(piece, BF16),
            pltpu.SemaphoreType.DMA((GROUPS, 4, chips)),
        )

    image, sums = pl.pallas_call(
        functools.partial(step_kernel, rows_n, cent_n),
        out_shape=(
            jax.ShapeDtypeStruct((part, OUTS), F32),
            jax.ShapeDtypeStruct((8, OUTS), F32),
        ),
        in_specs=[vmem, vmem, pl.BlockSpec(memory_space=pl.ANY), vmem, vmem],
        out_specs=(vmem, vmem),
        scratch_shapes=[
            pltpu.VMEM((chunks, CHUNK, precond.shape[1]), BF16),
            pltpu.SemaphoreType.DMA((chunks,)),
            pltpu.VMEM((chunks, CHUNK, rows_here), BF16),
            pltpu.VMEM((4 * FEAT, rows_here), BF16),
            pltpu.VMEM((2 * FEAT, rows_here), BF16),
            scan(chunks, (FEAT, CHUNK), I16, I16),
            scan(GROUPS * chunks, (group, CHUNK), F32, BF16),
            scan(GROUPS * chunks, (group, CHUNK), F32, BF16),
            pltpu.VMEM((OUTS, part), BF16),
            pltpu.VMEM((cent_n, OUTS, part), BF16),
            pltpu.VMEM((GROUPS, group, fit_part), BF16),
            pltpu.VMEM((GROUPS, cent_n, group, fit_part), BF16),
            pltpu.SemaphoreType.DMA((1 + GROUPS, 4, chips)),
            pltpu.VMEM((GROUPS, cent_n, group, fit_part), F32),
            scatter((group, fit_part)),
            pltpu.VMEM((GROUPS, cent_n, group, part), F32),
            scatter((group, part)),
            pltpu.VMEM((8, OUTS), F32),
            pltpu.VMEM((cent_n, 8, OUTS), F32),
            pltpu.VMEM((8, OUTS), F32),
            pltpu.VMEM((rows_n, 8, OUTS), F32),
            pltpu.SemaphoreType.DMA((4, max(cent_n, rows_n))),
        ],
        compiler_params=pltpu.CompilerParams(
            collective_id=0, has_side_effects=True, vmem_limit_bytes=67000000
        ),
        name="falkon_step",
    )(centre_index.reshape(chunks, 1, CHUNK), train_rows.T, precond, residual, direction)

    piece = jax.ShapeDtypeStruct((part, OUTS), F32)
    return pl.pallas_call(
        update_kernel,
        out_shape=(piece, piece, piece),
        in_specs=[vmem] * 5,
        out_specs=(vmem, vmem, vmem),
        name="falkon_update",
    )(sums, image, coefficients, residual, direction)


def solution(mesh):
    both = P(("rows", "cent"), None)
    return jax.shard_map(
        functools.partial(on_device, mesh.shape["rows"], mesh.shape["cent"]),
        mesh=mesh,
        in_specs=(P("rows", None), P("cent"), P("cent", "rows"), both, both, both),
        out_specs=(both, both, both),
        check_vma=False,
    )
```

time: 101 us -> 94.5 us (0.936)
  Pallas kernels: 101 us -> 93.7 us
    pallas_call x1, Pallas kernels: 98.3 us -> 91.5 us  [on_device(): pl.pallas_call(functools.partial(step_kernel, rows_n, cent_n), out_shape=...]
where the time goes in v1:
time: 94.5 us; the launch traced here: 94.3 us
  Pallas kernels  93.7 us (99%)
    pallas_call x1, Pallas kernels, on_device(): pl.pallas_call(functools.partial(step_kernel, rows_n, cent_n), out_shape=...  91.5 us
    pallas_call x1, Pallas kernels, on_device(): pl.pallas_call(update_kernel, out_shape=(piece, piece, piece), in_specs=[...  2.22 us

profile of v1, /device:TPU:0, one launch (start us, length us, event | category | flops | bytes accessed | tf_op | source)
XLA Modules:
  0.0 94.3 jit_solution(14107013748838088706)
XLA Ops:
  0.6 91.5 %falkon_step.1 = (f32[512,128]{1,0:T(8,128)}, f32[8,128]{1,0:T(8,128)}) custom-call(s32[8,1,256]{2,1,0:T(1,128)} %bitcast.3, f32[64,4096]{1,0:T(8,128)} %bitcast.2, bf16[2048,4096]{1,0:T(8,128)(2,1)} %p_hbm.1, f32[512,128]{1,0:T(8,128)} %res_ref.3, f32[512,128]{1,0:T(8,128)} %dir_ref.3), custom_call_target="tpu_custom_call" | custom-call | tf_op jit(solution)/shard_map/falkon_step/pallas_call | solution.py:537
  92.1 2.2 %falkon_update.1 = (f32[512,128]{1,0:T(8,128)}, f32[512,128]{1,0:T(8,128)}, f32[512,128]{1,0:T(8,128)}) custom-call(f32[8,128]{1,0:T(8,128)} %get-tuple-element.5.sums_ref, f32[512,128]{1,0:T(8,128)} %get-tuple-element.6.image_ref, f32[512,128]{1,0:T(8,128)} %coef_ref.1, f32[512,128]{1,0:T(8,128)} %res_ref.3, f32[512,128]{1,0:T(8,128)} %dir_ref.3), custom_call_target="tpu_custom_call" | custom-call | tf_op jit(solution)/shard_map/falkon_update/pallas_call | solution.py:576

commit v2 on v1

--- a/solution.py
+++ b/solution.py
@@ -12,9 +12,13 @@
 OUTS = 128
 CHUNK = 256
 GROUPS = 2
-LAG = 4
-COEF_AT = 10
-BUILD_AFTER = 8
+LAG = 5
+CUTS = (1, 5, 7)
+NEAR_AT = 8
+NEAR_SLOTS = 4
+FORWARD_BEFORE = 2
+COEF_AT = 12
+BUILD_AFTER = 0
 WIDEST = 6.0
 F32 = jnp.float32
 BF16 = jnp.bfloat16
@@ -58,9 +62,10 @@
 
 def step_kernel(
     rows_n, cent_n,
-    idx_ref, x_ref, p_hbm, res_ref, dir_ref,
+    idx_hbm, x_hbm, p_hbm, res_hbm, dir_hbm,
     image_ref, sums_ref,
-    p_buf, p_sem, kt_buf, xaug_t, nhl_t,
+    idx_ref, x_ref, res_ref, dir_ref, in_sems,
+    p_buf, p_sem, k_buf, xaug, xaug_t, caug_t, nhl_t,
     pick, coef, grad,
     dir_own, dir_all, fit_own, fit_all, gather_sems,
     fit_acc, fit_rs, img_acc, img_rs,
@@ -75,14 +80,28 @@
     chunks = p_buf.shape[0]
     rows_here = x_ref.shape[1]
     part = dir_own.shape[1]
-    fit_part = fit_acc.shape[3]
+    fit_part = fit_acc.shape[2]
     group = OUTS // GROUPS
     items = GROUPS * chunks
     last = rows_n - 1
     reach = LAG * last
 
+    near = chips - 1
+    paired = chips & (chips - 1) == 0
+
     def chip_at(distance):
-        return lax.rem(chip + distance, chips)
+        if not paired:
+            return lax.rem(chip + distance, chips)
+        at = chip
+        bit = 1
+        while bit < chips:
+            if distance & bit:
+                at = at + bit * (1 - 2 * lax.rem(lax.div(at, bit), 2))
+            bit *= 2
+        return at
+
+    def chip_from(distance):
+        return chip_at(distance) if paired else chip_at(chips - distance)
 
     def p_copy(k):
         return pltpu.make_async_copy(
@@ -99,10 +118,20 @@
             barrier, inc=1, device_id=(lax.rem(z + d, rows_n), me), device_id_type=MESH
         )
 
+    inputs = [
+        pltpu.make_async_copy(source, target, in_sems.at[at])
+        for at, (source, target) in enumerate(
+            ((dir_hbm, dir_ref), (x_hbm, x_ref), (idx_hbm, idx_ref), (res_hbm, res_ref))
+        )
+    ]
+    for copy in inputs:
+        copy.start()
+
     @pl.loop(0, chunks)
     def _(k):
         p_copy(k).start()
 
+    inputs[0].wait()
     dir_own[...] = dir_ref[...].T.astype(BF16)
     for scan in (pick, coef, grad):
         @pl.when(z == 0)
@@ -124,7 +153,7 @@
         )
 
     def forward_copy(which, whole, d):
-        source = chip_at(chips - d) * 2 + core
+        source = chip_from(d) * 2 + core
         return pltpu.make_async_remote_copy(
             src_ref=whole.at[source], dst_ref=whole.at[source],
             send_sem=gather_sems.at[which, 2, d], recv_sem=gather_sems.at[which, 3, d],
@@ -136,15 +165,17 @@
             gather_copy(which, own, whole, d).start()
         whole[me] = own[...]
 
-    def gather_forward(which, own, whole):
-        for d in range(1, chips):
+    def gather_forward(which, own, whole, distances):
+        for d in distances:
             gather_copy(which, own, whole, d).wait_recv()
             forward_copy(which, whole, d).start()
 
-    def gather_end(which, own, whole):
-        gather_copy(which, own, whole, 0).wait_recv()
-        for d in range(1, chips):
-            forward_copy(which, whole, d).wait_recv()
+    def gather_end(which, own, whole, distances):
+        for d in distances:
+            if d == 0:
+                gather_copy(which, own, whole, 0).wait_recv()
+            else:
+                forward_copy(which, whole, d).wait_recv()
 
     def gather_sent(which, own, whole):
         for d in range(chips):
@@ -236,24 +267,24 @@
             device_id=(z, chip_at(d) * 2 + core), device_id_type=MESH,
         )
 
-    def scatter_across(acc, buffers, g):
+    def scatter_across(mine, buffers, g):
         for d in list(range(1, chips)) + [0]:
             q = chip_at(d)
-            buffers[0][g, q] = acc[g, q * 2 + (1 - core)].astype(BF16)
+            buffers[0][g, q] = mine(g, q * 2 + (1 - core)).astype(BF16)
             across_copy(buffers, g, q).start()
 
-    def scatter_between(acc, buffers, g):
+    def scatter_between(mine, buffers, g):
         send_a, recv_a, send_b, recv_b, sems = buffers
         for d in range(1, chips):
             q = chip_at(d)
             across_copy(buffers, g, q).wait_recv()
-            send_b[g, d] = (acc[g, q * 2 + core] + recv_a[g, q].astype(F32)).astype(BF16)
+            send_b[g, d] = (mine(g, q * 2 + core) + recv_a[g, q].astype(F32)).astype(BF16)
             between_copy(buffers, g, d).start()
 
-    def scatter_end(acc, buffers, g):
+    def scatter_end(mine, buffers, g):
         send_a, recv_a, send_b, recv_b, sems = buffers
         across_copy(buffers, g, chip).wait_recv()
-        total = acc[g, me] + recv_a[g, chip].astype(F32)
+        total = mine(g, me) + recv_a[g, chip].astype(F32)
         for d in range(1, chips):
             between_copy(buffers, g, d).wait_recv()
             total = total + recv_b[g, d].astype(F32)
@@ -267,6 +298,9 @@
                 between_copy(buffers, g, d).wait_send()
 
     gather_start(0, dir_own, dir_all)
+    inputs[1].wait()
+    inputs[2].wait()
+    closer, farthest, every = range(1, near), range(near, chips), range(chips)
 
     x_block = rows_here // chunks
     for b in range(chunks):
@@ -284,6 +318,7 @@
         extra = augmented(high, low, POINT_NORM, 0, 3)
         for at, term in enumerate((high, low, high, extra)):
             xaug_t[at * FEAT : (at + 1) * FEAT, here] = term.astype(BF16)
+        xaug[here, :] = jnp.concatenate([high, low, high, extra], axis=0).T.astype(BF16)
 
     pick_block = math.gcd(rows_here, 1024)
 
@@ -296,37 +331,69 @@
             total = total + dot(nhl_t[:, b * pick_block : (b + 1) * pick_block], hot)
         pick[0][k] = (total[:FEAT] + total[FEAT:]).astype(I32).astype(I16)
 
-    def coef_own(k):
+    def coef_blocks(k, blocks):
+        total = jnp.zeros((OUTS, CHUNK), F32)
+        for block in blocks:
+            here = pl.ds(pl.multiple_of(block * part, part), part)
+            total = total + dot_t(dir_all[block], p_buf[k, :, here])
+        return total
+
+    def pair(d):
+        return [chip_from(d) * 2 + core, chip_from(d) * 2 + 1 - core]
+
+    def coef_near(k):
         p_copy(k).wait()
-        total = jnp.zeros((OUTS, CHUNK), F32)
-        for b in range(cent_n):
-            total = total + dot_t(dir_all[b], p_buf[k, :, b * part : (b + 1) * part])
+        total = coef_blocks(k, [me, other] + [b for d in closer for b in pair(d)])
         for g in range(GROUPS):
-            coef[0][g * chunks + k] = total[g * group : (g + 1) * group]
-
-    k_block = math.gcd(rows_here, 512)
+            coef[0][k * GROUPS + g] = total[g * group : (g + 1) * group]
+
+    def coef_far(k):
+        total = coef_blocks(k, [b for d in farthest for b in pair(d)])
+        for g in range(GROUPS):
+            coef[0][k * GROUPS + g] += total[g * group : (g + 1) * group]
+
+    fit_blocks = fit_part // CHUNK
 
     def build(k):
         number = scan_total(pick, k).astype(F32)
         high = number.astype(BF16).astype(F32)
         low = number - high
         extra = augmented(high, low, CENTRE_NORM, 3, 0)
-        caug = jnp.concatenate([high, high, low, extra], axis=0).T.astype(BF16)
-        for b in range(rows_here // k_block):
-            here = slice(b * k_block, (b + 1) * k_block)
-            kt_buf[k, :, here] = jnp.exp2(dot(caug, xaug_t[:, here])).astype(BF16)
-
-    def fit_add(i):
-        g = lax.div(i, chunks)
-        k = lax.rem(i, chunks)
-        low = scan_total(coef, i).astype(BF16)
+        caug = jnp.concatenate([high, high, low, extra], axis=0)
+        caug_t[k] = caug.astype(BF16)
+        caug = caug.T.astype(BF16)
+        for b in range(rows_here // CHUNK):
+            here = slice(b * CHUNK, (b + 1) * CHUNK)
+            k_buf[k, b] = jnp.exp2(dot(caug, xaug_t[:, here])).astype(BF16)
+
+    def rebuild(k):
+        for b in range(rows_here // CHUNK):
+            here = slice(b * CHUNK, (b + 1) * CHUNK)
+            k_buf[k, b] = jnp.exp2(dot(xaug[here, :], caug_t[k])).astype(BF16)
+
+    def fit_add(k):
+        low = jnp.concatenate(
+            [scan_total(coef, k * GROUPS + g).astype(BF16) for g in range(GROUPS)], axis=0
+        )
         for b in range(cent_n):
-            fit_acc[g, b] += dot(low, kt_buf[k, :, b * fit_part : (b + 1) * fit_part])
+            for h in range(fit_blocks):
+                here = slice(h * CHUNK, (h + 1) * CHUNK)
+                fit_acc[b, :, here] += dot(low, k_buf[k, b * fit_blocks + h])
+
+    def fit_mine(g, block):
+        return fit_acc[block, g * group : (g + 1) * group, :]
+
+    def img_mine(g, block):
+        return img_acc[g, block]
 
     fit_acc[...] = jnp.zeros_like(fit_acc)
     img_acc[...] = jnp.zeros_like(img_acc)
-    build_at = COEF_AT + BUILD_AFTER
+    build_at = max(COEF_AT + BUILD_AFTER, LAG * (last - 1))
     fit_at = COEF_AT + reach
+
+    def turn(it, start, phase):
+        step = it - start
+        return (step >= 0) & (step < items) & (lax.rem(step + items, GROUPS) == phase)
 
     @pl.loop(0, fit_at + items)
     def _(it):
@@ -340,48 +407,60 @@
         def _():
             augment_points(it)
 
-        @pl.when(it == COEF_AT)
-        def _():
-            gather_forward(0, dir_own, dir_all)
-            gather_end(0, dir_own, dir_all)
-
-        @pl.when((it >= COEF_AT) & (it < COEF_AT + chunks))
-        def _():
-            coef_own(it - COEF_AT)
+        for at, distances in ((NEAR_AT, closer), (COEF_AT, farthest)):
+            @pl.when(it == at - FORWARD_BEFORE)
+            def _():
+                gather_forward(0, dir_own, dir_all, distances)
+
+            @pl.when(it == at)
+            def _():
+                if at == NEAR_AT:
+                    gather_end(0, dir_own, dir_all, [0])
+                gather_end(0, dir_own, dir_all, distances)
+
+        @pl.when((it >= NEAR_AT) & (it < NEAR_AT + NEAR_SLOTS))
+        def _():
+            @pl.loop(0, chunks // NEAR_SLOTS)
+            def _(step):
+                coef_near((it - NEAR_AT) * (chunks // NEAR_SLOTS) + step)
+
+        @pl.when(turn(it, COEF_AT, 0))
+        def _():
+            coef_far(lax.div(it - COEF_AT, GROUPS))
 
         scan_step(coef, it - COEF_AT)
 
-        @pl.when((it >= build_at) & (it < build_at + chunks))
-        def _():
-            build(it - build_at)
-
-        @pl.when(it >= fit_at)
-        def _():
-            fit_add(it - fit_at)
-
-        for g in range(GROUPS):
-            done = fit_at + (g + 1) * chunks - 1
-
-            @pl.when(it == done)
-            def _():
-                scatter_across(fit_acc, fit_rs, g)
-
-            if g < GROUPS - 1:
-                @pl.when(it == done + 2)
-                def _():
-                    scatter_between(fit_acc, fit_rs, g)
+        @pl.when(turn(it, build_at, GROUPS - 1))
+        def _():
+            build(lax.div(it - build_at, GROUPS))
+
+        @pl.when(turn(it, fit_at, GROUPS - 1))
+        def _():
+            fit_add(lax.div(it - fit_at, GROUPS))
 
     def fit_shared(g):
-        fit_own[g] = scatter_end(fit_acc, fit_rs, g).astype(BF16)
+        fit_own[g] = scatter_end(fit_mine, fit_rs, g).astype(BF16)
         gather_start(1 + g, fit_own.at[g], fit_all.at[g])
 
-    for g in range(GROUPS - 1):
+    def rebuild_some(start, stop):
+        @pl.loop(start, stop)
+        def _(k):
+            rebuild(k)
+
+    cuts = [chunks * c // 8 for c in CUTS]
+    for g in range(GROUPS):
+        scatter_across(fit_mine, fit_rs, g)
+    rebuild_some(0, cuts[0])
+    for g in range(GROUPS):
+        scatter_between(fit_mine, fit_rs, g)
+    rebuild_some(cuts[0], cuts[1])
+    fit_shared(0)
+    rebuild_some(cuts[1], cuts[2])
+    for g in range(1, GROUPS):
         fit_shared(g)
-    scatter_between(fit_acc, fit_rs, GROUPS - 1)
-    for g in range(GROUPS - 1):
-        gather_forward(1 + g, fit_own.at[g], fit_all.at[g])
-    fit_shared(GROUPS - 1)
-    gather_end(1, fit_own.at[0], fit_all.at[0])
+    rebuild_some(cuts[2], chunks)
+    gather_forward(1, fit_own.at[0], fit_all.at[0], range(1, chips))
+    gather_end(1, fit_own.at[0], fit_all.at[0], every)
 
     scale = float(rows_here * rows_n) ** -0.5
 
@@ -390,7 +469,9 @@
         k = lax.rem(i, chunks)
         total = jnp.zeros((group, CHUNK), F32)
         for b in range(cent_n):
-            total = total + dot_t(fit_all[g, b], kt_buf[k, :, b * fit_part : (b + 1) * fit_part])
+            for h in range(fit_blocks):
+                here = slice(h * CHUNK, (h + 1) * CHUNK)
+                total = total + dot(fit_all[g, b, :, here], k_buf[k, b * fit_blocks + h])
         grad[0][i] = total
 
     def img_add(i):
@@ -402,12 +483,15 @@
 
     @pl.loop(0, items + reach)
     def _(it):
+        @pl.when(it == (GROUPS - 1) * chunks - FORWARD_BEFORE)
+        def _():
+            g = GROUPS - 1
+            gather_forward(1 + g, fit_own.at[g], fit_all.at[g], range(1, chips))
+
         for g in range(1, GROUPS):
             @pl.when(it == g * chunks)
             def _():
-                if g == GROUPS - 1:
-                    gather_forward(1 + g, fit_own.at[g], fit_all.at[g])
-                gather_end(1 + g, fit_own.at[g], fit_all.at[g])
+                gather_end(1 + g, fit_own.at[g], fit_all.at[g], every)
 
         @pl.when(it < items)
         def _():
@@ -424,16 +508,16 @@
 
             @pl.when(it == done)
             def _():
-                scatter_across(img_acc, img_rs, g)
+                scatter_across(img_mine, img_rs, g)
 
             if g < GROUPS - 1:
                 @pl.when(it == done + 2)
                 def _():
-                    scatter_between(img_acc, img_rs, g)
-
-    images = [scatter_end(img_acc, img_rs, g) for g in range(GROUPS - 1)]
-    scatter_between(img_acc, img_rs, GROUPS - 1)
-    images.append(scatter_end(img_acc, img_rs, GROUPS - 1))
+                    scatter_between(img_mine, img_rs, g)
+
+    images = [scatter_end(img_mine, img_rs, g) for g in range(GROUPS - 1)]
+    scatter_between(img_mine, img_rs, GROUPS - 1)
+    images.append(scatter_end(img_mine, img_rs, GROUPS - 1))
     image = jnp.concatenate(images, axis=0).T
     image = image + ridge_weight * dir_ref[...]
     image_ref[...] = image
@@ -441,6 +525,7 @@
     def rows_sum(value):
         return jnp.sum(value, axis=0, keepdims=True)
 
+    inputs[3].wait()
     residual = res_ref[...]
     sc_own[...] = jnp.concatenate(
         [
@@ -540,13 +625,20 @@
             jax.ShapeDtypeStruct((part, OUTS), F32),
             jax.ShapeDtypeStruct((8, OUTS), F32),
         ),
-        in_specs=[vmem, vmem, pl.BlockSpec(memory_space=pl.ANY), vmem, vmem],
+        in_specs=[pl.BlockSpec(memory_space=pl.ANY)] * 5,
         out_specs=(vmem, vmem),
         scratch_shapes=[
+            pltpu.VMEM((chunks, 1, CHUNK), I32),
+            pltpu.VMEM((FEAT, rows_here), F32),
+            pltpu.VMEM((part, OUTS), F32),
+            pltpu.VMEM((part, OUTS), F32),
+            pltpu.SemaphoreType.DMA((4,)),
             pltpu.VMEM((chunks, CHUNK, precond.shape[1]), BF16),
             pltpu.SemaphoreType.DMA((chunks,)),
-            pltpu.VMEM((chunks, CHUNK, rows_here), BF16),
+            pltpu.VMEM((chunks, rows_here // CHUNK, CHUNK, CHUNK), BF16),
+            pltpu.VMEM((rows_here, 4 * FEAT), BF16),
             pltpu.VMEM((4 * FEAT, rows_here), BF16),
+            pltpu.VMEM((chunks, 4 * FEAT, CHUNK), BF16),
             pltpu.VMEM((2 * FEAT, rows_here), BF16),
             scan(chunks, (FEAT, CHUNK), I16, I16),
             scan(GROUPS * chunks, (group, CHUNK), F32, BF16),
@@ -556,7 +648,7 @@
             pltpu.VMEM((GROUPS, group, fit_part), BF16),
             pltpu.VMEM((GROUPS, cent_n, group, fit_part), BF16),
             pltpu.SemaphoreType.DMA((1 + GROUPS, 4, chips)),
-            pltpu.VMEM((GROUPS, cent_n, group, fit_part), F32),
+            pltpu.VMEM((cent_n, OUTS, fit_part), F32),
             scatter((group, fit_part)),
             pltpu.VMEM((GROUPS, cent_n, group, part), F32),
             scatter((group, part)),

time: 94.5 us -> 92.5 us (0.979)
  Pallas kernels: 93.7 us -> 91.7 us
    pallas_call x1, Pallas kernels: 91.5 us -> 89.5 us  [on_device(): pl.pallas_call(functools.partial(step_kernel, rows_n, cent_n), out_shape=...]
where the time goes in v2:
time: 92.5 us; the launch traced here: 92.4 us
  Pallas kernels  91.7 us (99%)
    pallas_call x1, Pallas kernels, on_device(): pl.pallas_call(functools.partial(step_kernel, rows_n, cent_n), out_shape=...  89.5 us
    pallas_call x1, Pallas kernels, on_device(): pl.pallas_call(update_kernel, out_shape=(piece, piece, piece), in_specs=[...  2.22 us

profile of v2, /device:TPU:0, one launch (start us, length us, event | category | flops | bytes accessed | tf_op | source)
XLA Modules:
  0.0 92.4 jit_solution(9052307497854225241)
XLA Ops:
  0.6 89.5 %falkon_step.1 = (f32[512,128]{1,0:T(8,128)}, f32[8,128]{1,0:T(8,128)}) custom-call(s32[8,1,256]{2,1,0:T(1,128)} %bitcast.3, f32[64,4096]{1,0:T(8,128)} %bitcast.2, bf16[2048,4096]{1,0:T(8,128)(2,1)} %p_hbm.1, f32[512,128]{1,0:T(8,128)} %res_ref.1, f32[512,128]{1,0:T(8,128)} %dir_ref.1), custom_call_target="tpu_custom_call" | custom-call | tf_op jit(solution)/shard_map/falkon_step/pallas_call | solution.py:622
  90.2 2.2 %falkon_update.1 = (f32[512,128]{1,0:T(8,128)}, f32[512,128]{1,0:T(8,128)}, f32[512,128]{1,0:T(8,128)}) custom-call(f32[8,128]{1,0:T(8,128)} %get-tuple-element.5.sums_ref, f32[512,128]{1,0:T(8,128)} %get-tuple-element.6.image_ref, f32[512,128]{1,0:T(8,128)} %coef_ref.1, f32[512,128]{1,0:T(8,128)} %res_ref.1, f32[512,128]{1,0:T(8,128)} %dir_ref.1), custom_call_target="tpu_custom_call" | custom-call | tf_op jit(solution)/shard_map/falkon_update/pallas_call | solution.py:668

commit v3 on v2

--- a/solution.py
+++ b/solution.py
@@ -161,7 +161,8 @@
         )
 
     def gather_start(which, own, whole):
-        for d in list(range(1, chips)) + [0]:
+        order = range(1, chips) if which == 0 else range(chips - 1, 0, -1)
+        for d in [*order, 0]:
             gather_copy(which, own, whole, d).start()
         whole[me] = own[...]
 
@@ -268,14 +269,14 @@
         )
 
     def scatter_across(mine, buffers, g):
-        for d in list(range(1, chips)) + [0]:
+        for d in list(range(chips - 1, 0, -1)) + [0]:
             q = chip_at(d)
             buffers[0][g, q] = mine(g, q * 2 + (1 - core)).astype(BF16)
             across_copy(buffers, g, q).start()
 
     def scatter_between(mine, buffers, g):
         send_a, recv_a, send_b, recv_b, sems = buffers
-        for d in range(1, chips):
+        for d in range(chips - 1, 0, -1):
             q = chip_at(d)
             across_copy(buffers, g, q).wait_recv()
             send_b[g, d] = (mine(g, q * 2 + core) + recv_a[g, q].astype(F32)).astype(BF16)

time: 92.5 us -> 92.1 us (level)
  no operation moved by 1% of the time
where the time goes in v3:
time: 92.1 us; the launch traced here: 91.9 us
  Pallas kernels  91.3 us (99%)
    pallas_call x1, Pallas kernels, on_device(): pl.pallas_call(functools.partial(step_kernel, rows_n, cent_n), out_shape=...  89.1 us
    pallas_call x1, Pallas kernels, on_device(): pl.pallas_call(update_kernel, out_shape=(piece, piece, piece), in_specs=[...  2.22 us

profile of v3, /device:TPU:0, one launch (start us, length us, event | category | flops | bytes accessed | tf_op | source)
XLA Modules:
  0.0 91.9 jit_solution(2774916096649123146)
XLA Ops:
  0.6 89.1 %falkon_step.1 = (f32[512,128]{1,0:T(8,128)}, f32[8,128]{1,0:T(8,128)}) custom-call(s32[8,1,256]{2,1,0:T(1,128)} %bitcast.3, f32[64,4096]{1,0:T(8,128)} %bitcast.2, bf16[2048,4096]{1,0:T(8,128)(2,1)} %p_hbm.1, f32[512,128]{1,0:T(8,128)} %res_ref.1, f32[512,128]{1,0:T(8,128)} %dir_ref.1), custom_call_target="tpu_custom_call" | custom-call | tf_op jit(solution)/shard_map/falkon_step/pallas_call | solution.py:623
  89.7 2.2 %falkon_update.1 = (f32[512,128]{1,0:T(8,128)}, f32[512,128]{1,0:T(8,128)}, f32[512,128]{1,0:T(8,128)}) custom-call(f32[8,128]{1,0:T(8,128)} %get-tuple-element.5.sums_ref, f32[512,128]{1,0:T(8,128)} %get-tuple-element.6.image_ref, f32[512,128]{1,0:T(8,128)} %coef_ref.1, f32[512,128]{1,0:T(8,128)} %res_ref.1, f32[512,128]{1,0:T(8,128)} %dir_ref.1), custom_call_target="tpu_custom_call" | custom-call | tf_op jit(solution)/shard_map/falkon_update/pallas_call | solution.py:669
